TPU v7x, 128 devices: a whole 4x4x4 slice. The times are simulated.
128 devices in a mesh: defocus: 8 (over x_lo, y), blk: 16 (over z, x_hi, core).
Axes of the slice: x: 4 (x_hi: 2, x_lo: 2; x = x_hi * 2 + x_lo), y: 4, z: 4, core: 2. Of those that a mesh axis runs over, the one named last changes fastest.
Arguments:
- images: bfloat16 [8, 16, 384, 384], P('defocus', 'blk'), may hold values from -6 to 6
- projections: bfloat16 [16, 384, 384], P('blk', 'defocus'), may hold values from -6 to 6
- ctf_row: int32 [8, 16], P('defocus', 'blk'), may hold values from 0 to 63
- defocus_term: float32 [64], replicated, may hold values from 100 to 400
- astig_term: float32 [64], replicated, may hold values from -40 to 40
- astig_cross: float32 [64], replicated, may hold values from -40 to 40
- phase_shift: float32 [64], replicated, may hold values from 0.1 to 1.5
Outputs:
- peak: float32 [8, 16, 384, 384], P('defocus', 'blk')
All inputs are finite; a program needn't handle non-finite values.
Results may differ from a plain program's by a relative error of at most 0.0095.
Values may be sent and summed in bfloat16 or wider, within the bound.
No kernel may reach another device: no remote copies, remote signals or barrier semaphores. Data moves between devices by JAX's collectives and lax.ppermute only.
A program may use at most 64 MiB of HBM per device.

v0:
```python
import math
import jax
import jax.numpy as jnp
from jax import lax
from jax.sharding import PartitionSpec as P


def section_tables(pixels):
    indices = jnp.arange(pixels, dtype=jnp.int32)
    phases = indices[:, None] * indices[None, :] % pixels
    angles = phases.astype(jnp.float32) * (2.0 * math.pi / pixels)
    cosine_table = jnp.cos(angles).astype(jnp.bfloat16)
    sine_table = jnp.sin(angles).astype(jnp.bfloat16)
    boundary_table = jnp.concatenate([cosine_table, -sine_table], axis=1)
    squared_lookup = jnp.concatenate(
        [
            jnp.concatenate([cosine_table, sine_table], axis=1),
            jnp.concatenate([-sine_table, cosine_table], axis=1),
        ],
        axis=0,
    )
    return (boundary_table, squared_lookup)


def transform(template_stack, boundary_table, squared_lookup):
    pixels = template_stack.shape[-1]
    halves = jnp.einsum(
        "xgs,so->xgo", template_stack, boundary_table, preferred_element_type=jnp.float32
    ).astype(jnp.bfloat16)
    stacked = jnp.concatenate([halves[:, :, :pixels], halves[:, :, pixels:]], axis=1)
    result = jnp.einsum("ua,tab->tub", squared_lookup, stacked, preferred_element_type=jnp.float32)
    return (result[:, :pixels], result[:, pixels:])


def ctf_gains(row_ids, defocus_term, astig_term, astig_cross, phase_shift, pixels):
    indices = jnp.arange(pixels, dtype=jnp.int32)
    signed = jnp.where(indices < pixels // 2, indices, indices - pixels)
    frequency = signed.astype(jnp.float32) / pixels
    row_freq = frequency[:, None]
    col_freq = frequency[None, :]
    radial = row_freq * row_freq + col_freq * col_freq
    stretch = row_freq * row_freq - col_freq * col_freq
    skewed = 2.0 * row_freq * col_freq
    matches = row_ids[:, None] == jnp.arange(defocus_term.shape[0], dtype=jnp.int32)[None, :]

    def select_row(lookup_table):
        return jnp.sum(jnp.where(matches, lookup_table[None, :], 0.0), axis=1)[:, None, None]

    chi_angle = (
        select_row(defocus_term) * radial
        + select_row(astig_term) * stretch
        + select_row(astig_cross) * skewed
        + select_row(phase_shift)
    )
    return -jnp.sin(chi_angle)


def correlate(
    spectrum_re, spectrum_im, factor, ctf_weight, plane_re, plane_im, boundary_table, squared_lookup
):
    pixels = spectrum_re.shape[-1]
    wide_re = plane_re.astype(jnp.float32)
    wide_im = plane_im.astype(jnp.float32)
    template_norm = jnp.sum((wide_re * wide_re + wide_im * wide_im)[None] * ctf_weight, axis=(1, 2))
    scaling = factor / jnp.sqrt(template_norm + 1e-06)[:, None, None]
    product_re = ((spectrum_re * wide_re + spectrum_im * wide_im) * scaling).astype(jnp.bfloat16)
    product_im = ((spectrum_im * wide_re - spectrum_re * wide_im) * scaling).astype(jnp.bfloat16)
    combined_parts = jnp.concatenate([product_re, product_im], axis=2)
    halves = jnp.einsum(
        "xgs,so->xgo", combined_parts, squared_lookup, preferred_element_type=jnp.float32
    ).astype(jnp.bfloat16)
    stacked = jnp.concatenate([halves[:, :, :pixels], halves[:, :, pixels:]], axis=1)
    return jnp.einsum("ua,tab->tub", boundary_table, stacked, preferred_element_type=jnp.float32)


def per_device(images, projections, ctf_row, defocus_term, astig_term, astig_cross, phase_shift):
    micrographs = images[0]
    pixels = micrographs.shape[-1]
    boundary_table, squared_lookup = section_tables(pixels)
    spectrum_re, spectrum_im = transform(micrographs, boundary_table, squared_lookup)
    power_local = jnp.sum(spectrum_re * spectrum_re + spectrum_im * spectrum_im, axis=0)
    power_total = lax.psum(power_local.astype(jnp.bfloat16), "blk").astype(jnp.float32)
    mean_power = power_total / (lax.axis_size("blk") * micrographs.shape[0])
    noise_power = mean_power + 0.05 * jnp.mean(mean_power)
    transfer_gain = ctf_gains(
        ctf_row[0], defocus_term, astig_term, astig_cross, phase_shift, pixels
    )
    factor = transfer_gain / noise_power[None]
    ctf_weight = transfer_gain * factor
    library = lax.all_gather(projections, "defocus", axis=1, tiled=True)
    initial = jnp.full(micrographs.shape, -jnp.inf, jnp.float32)
    arrived_re, arrived_im = transform(
        lax.all_gather(library, "blk", axis=0, tiled=True), boundary_table, squared_lookup
    )
    rounded = lax.optimization_barrier(
        (arrived_re.astype(jnp.bfloat16), arrived_im.astype(jnp.bfloat16))
    )

    def one_plane(current, planes):
        scores = correlate(
            spectrum_re,
            spectrum_im,
            factor,
            ctf_weight,
            planes[0],
            planes[1],
            boundary_table,
            squared_lookup,
        )
        return (jnp.maximum(current, scores), None)

    result, _ = lax.scan(one_plane, initial, (rounded[0], rounded[1]))
    return result[None]


def solution(mesh):
    in_specs = (
        P("defocus", "blk", None, None),
        P("blk", "defocus", None),
        P("defocus", "blk"),
        P(),
        P(),
        P(),
        P(),
    )
    out_specs = P("defocus", "blk", None, None)
    return jax.shard_map(
        per_device, mesh=mesh, in_specs=in_specs, out_specs=out_specs, check_vma=False
    )
```

profile of v0, /device:TPU:1, one launch (start us, length us, event | category | flops | bytes accessed | tf_op | source)
XLA Modules:
  0.0 378.4 jit_solution(12518729024491444624)
XLA Ops:
  15.7 25.8 %all_gather.6 = bf16[1,384,384]{2,1,0:T(8,128)(2,1)} all-gather(bf16[1,48,384]{2,1,0:T(8,128)(2,1)S(1)} %copy-done.2), channel_id=1, replica_groups=mesh['defocus'=8,'blk'=16] {'defocus'}, dimensions={1}, use_global_device_ids=true | all-gather | bytes 331776 | tf_op jit(solution)/shard_map/all_gather | solution.py:90
  46.1 104.6 %all-reduce.2.cloned.1.call-done = bf16[384,384]{0,1:T(8,128)(2,1)} async-done(((bf16[384,384]{0,1:T(8,128)(2,1)}), bf16[384,384]{0,1:T(8,128)(2,1)}) %all-reduce.2.cloned.1.call-update) | async-done | bytes 294928 | tf_op jit(solution)/shard_map/psum | solution.py:82
  153.0 6.9 %fusion.43 = (f32[1,384,384]{1,2,0:T(8,128)}, f32[1,384,384]{1,2,0:T(8,128)S(1)}) fusion(f32[]{:T(128)S(6)} %mul_shard_map.3, bf16[384,384]{0,1:T(8,128)(2,1)} %all-reduce.2.cloned.1.call-done, f32[]{:T(128)} %get-tuple-element.152, f32[384]{0:T(512)S(1)} %get-tuple-element.157, f32[384]{0:T(512)S(1)} %get-tuple-element.156, f32[]{:T(128)} %get-tuple-element.153, ...), kind=kLoop, calls=%fused_computation.76 | loop fusion | flops 2211840 | bytes 1479188 | tf_op jit(solution)/shard_map/div | solution.py:88
  161.5 49.6 %all-gather.2.cloned.1.call-done = bf16[16,384,384]{2,1,0:T(8,128)(2,1)} async-done(((bf16[1,384,384]{2,1,0:T(8,128)(2,1)}), bf16[16,384,384]{2,1,0:T(8,128)(2,1)}) %all-gather.2.cloned.1.call-update) | async-done | bytes 4718608 | tf_op jit(solution)/shard_map/all_gather | solution.py:93
  211.0 9.7 %convert_bitcast_fusion.1 = bf16[16,384,768]{2,1,0:T(8,128)(2,1)} fusion(bf16[16,384,384]{2,1,0:T(8,128)(2,1)} %all-gather.2.cloned.1.call-done, bf16[384,384]{1,0:T(8,128)(2,1)S(1)} %fusion.36, bf16[384,384]{1,0:T(8,128)(2,1)S(1)} %cosine_convert_fusion), kind=kOutput, calls=%fused_computation.35 | convolution fusion | flops 3629776896 | bytes 14745600 | tf_op jit(solution)/shard_map/xgs,so->xgo/dot_general | solution.py:27
  220.8 7.3 %fusion.46 = (bf16[16,384,384]{2,1,0:T(8,128)(2,1)S(1)}, bf16[16,384,384]{2,1,0:T(8,128)(2,1)}) fusion(bf16[16,384,768]{2,1,0:T(8,128)(2,1)} %convert_bitcast_fusion.1), kind=kLoop, calls=%fused_computation.79 | loop fusion | bytes 18874368 | tf_op jit(solution)/shard_map/slice | solution.py:30
  228.1 11.7 %convert_bitcast_fusion = bf16[16,768,384]{1,2,0:T(8,128)(2,1)} fusion(bf16[16,384,384]{2,1,0:T(8,128)(2,1)} %get-tuple-element.144, bf16[16,384,384]{2,1,0:T(8,128)(2,1)S(1)} %get-tuple-element.143, bf16[384,384]{1,0:T(8,128)(2,1)S(1)} %cosine_convert_fusion, bf16[384,384]{1,0:T(8,128)(2,1)S(1)} %fusion.36, bf16[384,384]{1,0:T(8,128)(2,1)S(1)} %sine_convert_fusion), kind=kOutput, calls=%fused_computation.34 | convolution fusion | flops 7276068864 | bytes 19759104 | tf_op jit(solution)/shard_map/ua,tab->tub/dot_general | solution.py:31
  239.8 8.9 %fusion.45 = (bf16[16,384,384]{1,2,0:T(8,128)(2,1)}, bf16[16,384,384]{1,2,0:T(8,128)(2,1)}) fusion(bf16[16,768,384]{1,2,0:T(8,128)(2,1)} %convert_bitcast_fusion), kind=kLoop, calls=%fused_computation.78 | loop fusion | bytes 18874368 | tf_op jit(solution)/shard_map/slice | solution.py:32
  248.7 120.8 %while.11 = (s32[]{:T(128)}, f32[1,384,384]{1,2,0:T(8,128)}, bf16[16,384,384]{1,2,0:T(8,128)(2,1)}, f32[1,384,384]{2,1,0:T(8,128)S(1)}, bf16[16,384,384]{1,2,0:T...) while((s32[]{:T(128)}, f32[1,384,384]{1,2,0:T(8,128)}, ...), condition=%wide.region_8.9_spmd.clone, body=%wide.region_6.8_spmd.clone.sunk | while | flops 685375488 | bytes 17105100 | solution.py:112
  261.0 2.6 fusion.64
  268.6 2.6 fusion.64
  276.2 2.6 fusion.64
  283.7 2.6 fusion.64
  291.3 2.6 fusion.64
  298.8 2.6 fusion.64
  306.4 2.6 fusion.64
  314.0 2.6 fusion.64
  321.5 2.6 fusion.64
  329.1 2.6 fusion.64
  336.6 2.6 fusion.64
  344.2 2.6 fusion.64
  351.8 2.6 fusion.64
  359.3 2.6 fusion.64
  366.9 2.6 fusion.64
  (181 shorter events, 88.6 us)
Async XLA Ops:
  6.5 7.0 %copy-start = (bf16[1,1,384,384]{3,2,1,0:T(8,128)(2,1)S(1)}, bf16[1,1,384,384]{3,2,1,0:T(8,128)(2,1)}, u32[]{:S(2)}) copy-start(bf16[1,1,384,384]{3,2,1,0:T(8,128)(2,1)} %param.9) | copy-start | bytes 884740
  6.5 144.1 %all-reduce.2.cloned.1.call-start = ((), (), s32[]{:S(2)}) async-start(), calls=%async_computation.1 | async-start | bytes 589824 | tf_op jit(solution)/shard_map/psum | solution.py:82
  14.7 1.0 copy-start.2
  14.8 27.9 %copy-start.3 = (f32[64]{0:T(128)S(1)}, f32[64]{0:T(128)}, u32[]{:S(2)}) copy-start(f32[64]{0:T(128)} %param.15) | copy-start | bytes 772
  14.8 27.9 %copy-start.4 = (f32[64]{0:T(128)S(1)}, f32[64]{0:T(128)}, u32[]{:S(2)}) copy-start(f32[64]{0:T(128)} %param.14) | copy-start | bytes 772
  14.8 28.6 %copy-start.5 = (f32[64]{0:T(128)S(1)}, f32[64]{0:T(128)}, u32[]{:S(2)}) copy-start(f32[64]{0:T(128)} %param.13) | copy-start | bytes 772
  14.8 28.6 %copy-start.6 = (f32[64]{0:T(128)S(1)}, f32[64]{0:T(128)}, u32[]{:S(2)}) copy-start(f32[64]{0:T(128)} %param.12) | copy-start | bytes 772
  15.7 195.4 %all-gather.2.cloned.1.call-start = ((), (), s32[]{:S(2)}) async-start(), calls=%async_computation | async-start | bytes 5013504 | tf_op jit(solution)/shard_map/all_gather | solution.py:93
  251.7 1.3 copy-start.1
  259.1 1.3 copy-start.1
  266.6 1.3 copy-start.1
  274.2 1.3 copy-start.1
  281.7 1.3 copy-start.1
  289.3 1.3 copy-start.1
  296.9 1.3 copy-start.1
  304.4 1.3 copy-start.1
  312.0 1.3 copy-start.1
  319.5 1.3 copy-start.1
  327.1 1.3 copy-start.1
  334.7 1.3 copy-start.1
  342.2 1.3 copy-start.1
  349.8 1.3 copy-start.1
  357.3 1.3 copy-start.1
  364.9 1.3 copy-start.1
Sparse Core Ops, SparseCore 0:
  15.8 134.7 all-reduce.1
  153.4 57.6 all-gather.1
where the time goes:
time: 380 us; the launch traced here: 378 us
  waiting for transfers between devices  154 us (41%)
  matrix products  73.6 us (19%)
  local copies, waits for them, and re-layouts  62.3 us (16%)
  other arithmetic  35.8 us (9%)
  blocking collectives  25.8 us (7%)
  between operations  14.9 us (4%)
  loops' own time  11.8 us (3%)
    psum x1, waiting for transfers between devices, per_device(): lax.psum(power_local.astype(jnp.bfloat16), 'blk').astype(jnp.float32)  105 us
    all_gather x1, waiting for transfers between devices, per_device(): lax.all_gather(library, 'blk', axis=0, tiled=True)  49.6 us
    dot_general x16, matrix products, correlate(): jnp.einsum('ua,tab->tub', boundary_table, stacked, preferred_element_type...  41 us
    all_gather x1, blocking collectives, per_device(): library = lax.all_gather(projections, 'defocus', axis=1, tiled=True)  25.8 us
    dynamic_slice x48, local copies, waits for them, and re-layouts, per_device(): result, _ = lax.scan(one_plane, initial, (rounded[0], rounded[1]))  24.7 us
    while x32, local copies, waits for them, and re-layouts  16.2 us
    dot_general x2, matrix products, transform(): jnp.einsum('ua,tab->tub', squared_lookup, stacked, preferred_element_type...  12.4 us
    reduce_sum x16, other arithmetic, correlate(): jnp.sum((wide_re * wide_re + wide_im * wide_im)[None] * ctf_weight, axis=...  12.1 us
  transfers between devices with their start and end apart: 2, of which 2 were waited for; matrix products, arithmetic and copies ran while one was open for 4% of the time, Pallas kernels for 0%

commit v1 on v0

--- a/solution.py
+++ b/solution.py
@@ -3,6 +3,12 @@
 import jax.numpy as jnp
 from jax import lax
 from jax.sharding import PartitionSpec as P
+
+
+def summed_here(x, axis):
+    parts = lax.all_gather(x, axis, axis=0, tiled=False)
+    result = parts.sum(axis=0)
+    return result
 
 
 def section_tables(pixels):
@@ -79,7 +85,7 @@
     boundary_table, squared_lookup = section_tables(pixels)
     spectrum_re, spectrum_im = transform(micrographs, boundary_table, squared_lookup)
     power_local = jnp.sum(spectrum_re * spectrum_re + spectrum_im * spectrum_im, axis=0)
-    power_total = lax.psum(power_local.astype(jnp.bfloat16), "blk").astype(jnp.float32)
+    power_total = summed_here(power_local.astype(jnp.bfloat16), "blk").astype(jnp.float32)
     mean_power = power_total / (lax.axis_size("blk") * micrographs.shape[0])
     noise_power = mean_power + 0.05 * jnp.mean(mean_power)
     transfer_gain = ctf_gains(

time: 380 us -> 297 us (0.78)
  waiting for transfers between devices: 154 us -> 72.8 us
    psum x1 -> x0, waiting for transfers between devices: 105 us -> none  [per_device(): lax.psum(power_local.astype(jnp.bfloat16), 'blk').astype(jnp.float32)]
    all_gather x0 -> x1, waiting for transfers between devices: none -> 20.2 us  [summed_here(): parts = lax.all_gather(x, axis, axis=0, tiled=False)]
  transfers between devices with their start and end apart: 2 -> 2, of which waited for: 2 -> 2; matrix products, arithmetic and copies ran while one was open for 4% -> 17% of each run, Pallas kernels for 0% -> 0%
where the time goes in v1:
time: 297 us; the launch traced here: 296 us
  matrix products  74.5 us (25%)
  waiting for transfers between devices  72.8 us (25%)
  local copies, waits for them, and re-layouts  62.5 us (21%)
  other arithmetic  34.6 us (12%)
  blocking collectives  25.8 us (9%)
  between operations  14.8 us (5%)
  loops' own time  10.6 us (4%)
    all_gather x1, waiting for transfers between devices, per_device(): lax.all_gather(library, 'blk', axis=0, tiled=True)  52.6 us
    dot_general x16, matrix products, correlate(): jnp.einsum('ua,tab->tub', boundary_table, stacked, preferred_element_type...  42 us
    all_gather x1, blocking collectives, per_device(): library = lax.all_gather(projections, 'defocus', axis=1, tiled=True)  25.8 us
    dynamic_slice x48, local copies, waits for them, and re-layouts, per_device(): result, _ = lax.scan(one_plane, initial, (rounded[0], rounded[1]))  24.7 us
    all_gather x1, waiting for transfers between devices, summed_here(): parts = lax.all_gather(x, axis, axis=0, tiled=False)  20.2 us
    while x32, local copies, waits for them, and re-layouts  16.2 us
    dot_general x2, matrix products, transform(): jnp.einsum('ua,tab->tub', squared_lookup, stacked, preferred_element_type...  12.4 us
    reduce_sum x16, other arithmetic, correlate(): jnp.sum((wide_re * wide_re + wide_im * wide_im)[None] * ctf_weight, axis=...  12 us
  transfers between devices with their start and end apart: 2, of which 2 were waited for; matrix products, arithmetic and copies ran while one was open for 17% of the time, Pallas kernels for 0%

profile of v1, /device:TPU:1, one launch (start us, length us, event | category | flops | bytes accessed | tf_op | source)
XLA Modules:
  0.0 295.8 jit_solution(8910089067790283671)
XLA Ops:
  6.5 25.8 %all_gather.10 = bf16[1,384,384]{2,1,0:T(8,128)(2,1)} all-gather(bf16[1,48,384]{2,1,0:T(8,128)(2,1)} %param.10), channel_id=1, replica_groups=mesh['defocus'=8,'blk'=16] {'defocus'}, dimensions={1}, use_global_device_ids=true | all-gather | bytes 331776 | tf_op jit(solution)/shard_map/all_gather | solution.py:96
  46.1 52.6 %all-gather.3.cloned.1.call-done = bf16[16,384,384]{2,1,0:T(8,128)(2,1)} async-done(((bf16[1,384,384]{2,1,0:T(8,128)(2,1)}), bf16[16,384,384]{2,1,0:T(8,128)(2,1)}) %all-gather.3.cloned.1.call-update) | async-done | bytes 4718608 | tf_op jit(solution)/shard_map/all_gather | solution.py:99
  98.7 9.7 %convert_bitcast_fusion.1 = bf16[16,384,768]{2,1,0:T(8,128)(2,1)} fusion(bf16[16,384,384]{2,1,0:T(8,128)(2,1)} %all-gather.3.cloned.1.call-done, bf16[384,384]{1,0:T(8,128)(2,1)S(1)} %fusion.36, bf16[384,384]{1,0:T(8,128)(2,1)S(1)} %cosine_convert_fusion), kind=kOutput, calls=%fused_computation.35 | convolution fusion | flops 3629776896 | bytes 14745600 | tf_op jit(solution)/shard_map/xgs,so->xgo/dot_general | solution.py:33
  108.4 7.4 %fusion.45 = (bf16[16,384,384]{2,1,0:T(8,128)(2,1)S(1)}, bf16[16,384,384]{2,1,0:T(8,128)(2,1)}) fusion(bf16[16,384,768]{2,1,0:T(8,128)(2,1)} %convert_bitcast_fusion.1), kind=kLoop, calls=%fused_computation.77 | loop fusion | bytes 18874368 | tf_op jit(solution)/shard_map/slice | solution.py:36
  115.8 11.7 %convert_bitcast_fusion = bf16[16,768,384]{1,2,0:T(8,128)(2,1)} fusion(bf16[16,384,384]{2,1,0:T(8,128)(2,1)} %get-tuple-element.144, bf16[16,384,384]{2,1,0:T(8,128)(2,1)S(1)} %get-tuple-element.143, bf16[384,384]{1,0:T(8,128)(2,1)S(1)} %cosine_convert_fusion, bf16[384,384]{1,0:T(8,128)(2,1)S(1)} %fusion.36, bf16[384,384]{1,0:T(8,128)(2,1)S(1)} %sine_convert_fusion), kind=kOutput, calls=%fused_computation.34 | convolution fusion | flops 7276068864 | bytes 19759104 | tf_op jit(solution)/shard_map/ua,tab->tub/dot_general | solution.py:37
  127.6 9.0 %fusion.44 = (bf16[16,384,384]{1,2,0:T(8,128)(2,1)}, bf16[16,384,384]{1,2,0:T(8,128)(2,1)}) fusion(bf16[16,768,384]{1,2,0:T(8,128)(2,1)} %convert_bitcast_fusion), kind=kLoop, calls=%fused_computation.76 | loop fusion | bytes 18874368 | tf_op jit(solution)/shard_map/slice | solution.py:38
  136.5 20.2 %all-gather.5.cloned.1.call-done = bf16[16,384,384]{2,1,0:T(8,128)(2,1)} async-done(((bf16[1,384,384]{2,1,0:T(8,128)(2,1)}), bf16[16,384,384]{2,1,0:T(8,128)(2,1)}) %all-gather.5.cloned.1.call-update) | async-done | bytes 4718608 | tf_op jit(solution)/shard_map/all_gather | solution.py:9
  156.7 3.1 %reduce_sum.74 = bf16[384,384]{1,0:T(8,128)(2,1)S(1)} reduce(bf16[16,384,384]{2,1,0:T(8,128)(2,1)} %all-gather.5.cloned.1.call-done, bf16[]{:T(256)} %constant.50.clone.1), dimensions={0}, to_apply=%region_4.5 | reduce | flops 2211840 | bytes 5013506 | tf_op jit(solution)/shard_map/reduce_sum | solution.py:10
  161.3 4.6 %bitcast_divide_fusion = (f32[1,384,384]{1,2,0:T(8,128)S(1)}, f32[1,384,384]{1,2,0:T(8,128)S(1)}) fusion(bf16[384,384]{0,1:T(8,128)(2,1)S(1)} %copy.27, f32[]{:T(128)S(6)} %mul_shard_map.3, f32[]{:T(128)} %get-tuple-element.152, f32[384]{0:T(512)S(1)} %get-tuple-element.157, f32[384]{0:T(512)S(1)} %get-tuple-element.156, f32[]{:T(128)} %get-tuple-element.153, ...), kind=kLoop, calls=%fused_computation.48 | loop fusion | flops 2211840 | bytes 1479188 | tf_op jit(solution)/shard_map/div | solution.py:94
  166.4 120.3 %while.11 = (s32[]{:T(128)}, f32[1,384,384]{1,2,0:T(8,128)}, bf16[16,384,384]{1,2,0:T(8,128)(2,1)}, f32[1,384,384]{2,1,0:T(8,128)S(1)}, bf16[16,384,384]{1,2,0:T...) while((s32[]{:T(128)}, f32[1,384,384]{1,2,0:T(8,128)}, ...), condition=%wide.region_8.9_spmd.clone, body=%wide.region_6.8_spmd.clone.sunk | while | flops 685375488 | bytes 17105100 | solution.py:118
  178.7 2.6 fusion.63
  186.2 2.6 fusion.63
  193.8 2.6 fusion.63
  201.3 2.6 fusion.63
  208.8 2.6 fusion.63
  216.4 2.6 fusion.63
  223.9 2.6 fusion.63
  231.4 2.6 fusion.63
  239.0 2.6 fusion.63
  246.5 2.6 fusion.63
  254.0 2.6 fusion.63
  261.6 2.6 fusion.63
  276.6 2.6 fusion.63
  284.2 2.6 fusion.63
  (182 shorter events, 89.4 us)
Async XLA Ops:
  6.5 32.8 %copy-start = (bf16[1,1,384,384]{3,2,1,0:T(8,128)(2,1)S(1)}, bf16[1,1,384,384]{3,2,1,0:T(8,128)(2,1)}, u32[]{:S(2)}) copy-start(bf16[1,1,384,384]{3,2,1,0:T(8,128)(2,1)} %param.9) | copy-start | bytes 884740
  6.5 92.2 %all-gather.3.cloned.1.call-start = ((), (), s32[]{:S(2)}) async-start(), calls=%async_computation | async-start | bytes 5013504 | tf_op jit(solution)/shard_map/all_gather | solution.py:99
  32.4 124.3 %all-gather.5.cloned.1.call-start = ((), (), s32[]{:S(2)}) async-start(), calls=%async_computation.1 | async-start | bytes 5013504 | tf_op jit(solution)/shard_map/all_gather | solution.py:9
  40.6 2.3 copy-start.2
  40.6 2.3 copy-start.3
  40.6 2.9 copy-start.4
  40.6 2.9 copy-start.5
  169.4 1.3 copy-start.1
  176.7 1.3 copy-start.1
  184.3 1.3 copy-start.1
  191.8 1.3 copy-start.1
  199.3 1.3 copy-start.1
  206.9 1.3 copy-start.1
  214.4 1.3 copy-start.1
  221.9 1.3 copy-start.1
  229.5 1.3 copy-start.1
  237.0 1.3 copy-start.1
  244.5 1.3 copy-start.1
  252.1 1.3 copy-start.1
  259.6 1.3 copy-start.1
  267.1 1.3 copy-start.1
  274.6 1.3 copy-start.1
  282.2 1.3 copy-start.1
Sparse Core Ops, SparseCore 0:
  32.5 66.2 all-gather.2
  101.2 55.4 all-gather.4
